TPU v7x, 256 devices: a whole 4x4x8 slice. The times are simulated.
256 devices in a mesh: tm: 8 (over y, x_hi), space: 32 (over z, x_lo, core).
Axes of the slice: x: 4 (x_hi: 2, x_lo: 2; x = x_hi * 2 + x_lo), y: 4, z: 8, core: 2. Of those that a mesh axis runs over, the one named last changes fastest.
Arguments:
- wave_field: bfloat16 [16, 8192, 256], P('tm', 'space'), may hold values from -600 to 600
- cotangent: bfloat16 [16, 8192, 256], P('tm', 'space'), may hold values from -6 to 6
- block_lists: int32 [16, 64, 4], P('tm', 'space'), may hold values from 0 to 63, as said below
- project_weights: bfloat16 [2, 256, 768], replicated, may hold values from -2 to 2
- combine_weights: bfloat16 [2, 256, 256], replicated, may hold values from -0.375 to 0.375
Outputs:
- mixed_field: bfloat16 [16, 8192, 256], P('tm', 'space')
- field_grad: bfloat16 [16, 8192, 256], P('tm', 'space')
- project_grad: float32 [2, 256, 768], replicated
- combine_grad: float32 [2, 256, 256], replicated
Inputs may be any that keep to these rules, and one draw needn't show every extreme that they name: `block_lists`: for frame f and block b, entry 0 is b itself, entry 1 is b - 2 or b + 2, and every entry lies within 2 blocks of b; entries may repeat.
All inputs are finite; a program needn't handle non-finite values.
Results may differ from a plain program's by a relative error of at most 0.012.
Values may be sent and summed in bfloat16 or wider, within the bound.
A program may use at most 128 MiB of HBM per device.

v0:
```python
import math
import jax
import jax.numpy as jnp
from jax import lax
from jax.sharding import PartitionSpec as P

HEADS = 8
BLOCK = 128
HREACH = 2
epsilon = 1e-05


def with_halo(cells, sides, width):
    for axis, dim in sides:
        count = lax.axis_size(axis)
        ends = count - 1
        head = lax.slice_in_dim(cells, 0, width, axis=dim)
        tail = lax.slice_in_dim(cells, cells.shape[dim] - width, cells.shape[dim], axis=dim)
        cells = jnp.concatenate(
            [
                lax.ppermute(tail, axis, [(i, (i + 1) % count) for i in range(ends)]),
                cells,
                lax.ppermute(head, axis, [((i + 1) % count, i) for i in range(ends)]),
            ],
            axis=dim,
        )
    return cells


def layer_norm(tok_rows):
    widened = tok_rows.astype(jnp.float32)
    centered = widened - jnp.mean(widened, axis=-1, keepdims=True)
    inverse = lax.rsqrt(jnp.mean(centered * centered, axis=-1, keepdims=True) + epsilon)
    return (centered * inverse, inverse)


def norm_backward(upstream, normed, inverse):
    mean_grad = jnp.mean(upstream, axis=-1, keepdims=True)
    mean_cross = jnp.mean(upstream * normed, axis=-1, keepdims=True)
    return inverse * (upstream - mean_grad - normed * mean_cross)


def matmul(left_op, right_op):
    return jnp.dot(left_op, right_op, preferred_element_type=jnp.float32)


def wide_dot(left_op, right_op):
    return jnp.dot(
        left_op.astype(jnp.float32), right_op.astype(jnp.float32), precision=lax.Precision.HIGHEST
    )


def matmul_left(left_op, right_op):
    return lax.dot_general(
        left_op, right_op, (((0,), (0,)), ((), ())), preferred_element_type=jnp.float32
    )


def matmul_right(left_op, right_op):
    return lax.dot_general(
        left_op, right_op, (((1,), (1,)), ((), ())), preferred_element_type=jnp.float32
    )


def einsum_wide(formula, left_op, right_op):
    return jnp.einsum(formula, left_op, right_op, preferred_element_type=jnp.float32)


def softmax_rows(scores, reduce_axis):
    row_max = jnp.max(scores, axis=reduce_axis, keepdims=True)
    exp_scores = jnp.exp(scores - row_max)
    return lax.optimization_barrier(
        (exp_scores / jnp.sum(exp_scores, axis=reduce_axis, keepdims=True)).astype(jnp.bfloat16)
    )


def temporal_pair(tok_rows, cot_rows, project, combine, score_scale):
    frame_count, row_count, features = tok_rows.shape
    head_width = features // HEADS
    normed, inverse = layer_norm(tok_rows)
    normed_act = normed.astype(jnp.bfloat16).reshape(frame_count * row_count, features)
    projected = (
        matmul(normed_act, project)
        .astype(jnp.bfloat16)
        .reshape(frame_count, row_count, 3, HEADS, head_width)
    )
    queries = projected[:, :, 0]
    key_part = projected[:, :, 1]
    value_part = projected[:, :, 2]
    attn_probs = softmax_rows(einsum_wide("frhe,grhe->hfgr", queries, key_part) * score_scale, 2)
    attended = (
        einsum_wide("hfgr,grhe->frhe", attn_probs, value_part)
        .astype(jnp.bfloat16)
        .reshape(frame_count * row_count, features)
    )
    mixed = (
        tok_rows.astype(jnp.float32)
        + matmul(attended, combine).reshape(frame_count, row_count, features)
    ).astype(jnp.bfloat16)
    flat_cot = cot_rows.reshape(frame_count * row_count, features)
    outward = matmul_left(attended, flat_cot)
    attn_grad = (
        matmul_right(flat_cot, combine)
        .astype(jnp.bfloat16)
        .reshape(frame_count, row_count, HEADS, head_width)
    )
    grad_probs = einsum_wide("frhe,grhe->hfgr", attn_grad, value_part)
    prob_wide = attn_probs.astype(jnp.float32)
    row_delta = jnp.sum(prob_wide * grad_probs, axis=2, keepdims=True)
    grad_scores = (prob_wide * (grad_probs - row_delta) * score_scale).astype(jnp.bfloat16)
    grad_query = einsum_wide("hfgr,grhe->frhe", grad_scores, key_part)
    grad_keys = einsum_wide("hfgr,frhe->grhe", grad_scores, queries)
    grad_values = einsum_wide("hfgr,frhe->grhe", attn_probs, attn_grad)
    project_rows = (
        jnp.stack([grad_query, grad_keys, grad_values], axis=2)
        .astype(jnp.bfloat16)
        .reshape(frame_count * row_count, 3 * features)
    )
    inward = matmul_left(normed_act, project_rows)
    act_grad = matmul_right(project_rows, project).reshape(frame_count, row_count, features)
    field_rows = (cot_rows.astype(jnp.float32) + norm_backward(act_grad, normed, inverse)).astype(
        jnp.bfloat16
    )
    return (mixed, field_rows, inward, outward)


def owner_sums(tile_sums, edge_sums, rim_rows, row_count):
    arrived = with_halo(edge_sums.astype(jnp.bfloat16), (("space", 1),), rim_rows).astype(
        edge_sums.dtype
    )
    pair_grad = tile_sums[:, rim_rows : rim_rows + row_count]
    pair_grad = pair_grad + arrived[:, :rim_rows]
    pair_grad = pair_grad + arrived[:, 3 * rim_rows :]
    return pair_grad


def per_device(wave_field, cotangent, block_lists, project_weights, combine_weights):
    frame_count, row_count, features = wave_field.shape
    head_width = features // HEADS
    score_scale = 1.0 / math.sqrt(head_width)
    block_count = row_count // BLOCK
    list_length = block_lists.shape[-1]
    rim_rows = HREACH * BLOCK
    padded_blocks = block_count + 2 * HREACH
    group_count = frame_count * block_count // 4
    space_project = project_weights[0]
    space_combine = combine_weights[0]
    normed, inverse = layer_norm(wave_field)
    normed_act = normed.astype(jnp.bfloat16)
    flat_act = normed_act.reshape(frame_count * row_count, features)
    projected = (
        matmul(flat_act, space_project)
        .astype(jnp.bfloat16)
        .reshape(frame_count, row_count, 3 * features)
    )
    keys_values = projected[:, :, features:]
    extended = with_halo(keys_values, (("space", 1),), rim_rows)
    first_block = lax.axis_index("space") * block_count - HREACH
    frame_base = (jnp.arange(frame_count, dtype=jnp.int32) * padded_blocks)[:, None, None]
    group_index = (block_lists - first_block + frame_base).reshape(group_count, 4 * list_length)
    padded_flat = extended.reshape(frame_count * padded_blocks, BLOCK, 2, HEADS, head_width)
    queries = projected[:, :, :features].reshape(group_count, 4, BLOCK, HEADS, head_width)

    def group_weights(group_query, group_rows):
        picked = jnp.take(padded_flat, group_rows, axis=0).reshape(
            4, list_length * BLOCK, 2, HEADS, head_width
        )
        scores = einsum_wide("gqhe,gkhe->ghqk", group_query, picked[:, :, 0]) * score_scale
        return (picked, softmax_rows(scores, 3))

    def forward_group(element):
        picked, attn_probs = group_weights(element[0], element[1])
        return einsum_wide("ghqk,gkhe->gqhe", attn_probs, picked[:, :, 1]).astype(jnp.bfloat16)

    attended = lax.map(forward_group, (queries, group_index)).reshape(
        frame_count * row_count, features
    )
    mixed_space = (
        wave_field.astype(jnp.float32)
        + matmul(attended, space_combine).reshape(frame_count, row_count, features)
    ).astype(jnp.bfloat16)
    history, history_cot = (
        lax.all_to_all(mixed_space, "tm", split_axis=1, concat_axis=0, tiled=True),
        lax.all_to_all(cotangent, "tm", split_axis=1, concat_axis=0, tiled=True),
    )
    time_mixed, time_grad, time_inward, time_outward = temporal_pair(
        history, history_cot, project_weights[1], combine_weights[1], score_scale
    )
    mixed_field, mixed_grad = (
        lax.all_to_all(time_mixed, "tm", split_axis=0, concat_axis=1, tiled=True),
        lax.all_to_all(time_grad, "tm", split_axis=0, concat_axis=1, tiled=True),
    )
    flat_grad = mixed_grad.reshape(frame_count * row_count, features)
    space_outward = matmul_left(attended, flat_grad)
    attn_grad = (
        matmul_right(flat_grad, space_combine)
        .astype(jnp.bfloat16)
        .reshape(group_count, 4, BLOCK, HEADS, head_width)
    )

    def backward_group(running, element):
        group_query, group_rows, group_grad = element
        picked, attn_probs = group_weights(group_query, group_rows)
        key_part = picked[:, :, 0]
        value_part = picked[:, :, 1]
        prob_wide = attn_probs.astype(jnp.float32)
        grad_probs = einsum_wide("gqhe,gkhe->ghqk", group_grad, value_part)
        row_delta = jnp.sum(prob_wide * grad_probs, axis=3, keepdims=True)
        grad_scores = (prob_wide * (grad_probs - row_delta) * score_scale).astype(jnp.bfloat16)
        grad_query = einsum_wide("ghqk,gkhe->gqhe", grad_scores, key_part).astype(jnp.bfloat16)
        grad_keys = einsum_wide("ghqk,gqhe->gkhe", grad_scores, group_query)
        grad_values = einsum_wide("ghqk,gqhe->gkhe", attn_probs, group_grad)
        key_tiles = jnp.stack([grad_keys, grad_values], axis=2).reshape(
            4 * list_length, BLOCK * 2 * features
        )
        return (running.at[group_rows].add(key_tiles), grad_query)

    zero_tiles = jnp.zeros((frame_count * padded_blocks, BLOCK * 2 * features), jnp.float32)
    tile_sums, grad_query = lax.scan(backward_group, zero_tiles, (queries, group_index, attn_grad))
    tile_sums = tile_sums.reshape(frame_count, row_count + 2 * rim_rows, 2 * features)
    edge_sums = jnp.concatenate(
        [tile_sums[:, :rim_rows], tile_sums[:, rim_rows + row_count :]], axis=1
    )
    kv_project = space_project[:, features:]
    query_flat = grad_query.reshape(frame_count * row_count, features)
    pair_grad = owner_sums(tile_sums, edge_sums, rim_rows, row_count)
    pair_flat = pair_grad.reshape(frame_count * row_count, 2 * features)
    space_inward = jnp.concatenate(
        [matmul_left(flat_act, query_flat), wide_dot(flat_act.T, pair_flat)], axis=1
    )
    act_grad = matmul_right(query_flat, space_project[:, :features]) + wide_dot(
        pair_flat, kv_project.T
    )
    act_grad = act_grad.reshape(frame_count, row_count, features)
    field_grad = (mixed_grad.astype(jnp.float32) + norm_backward(act_grad, normed, inverse)).astype(
        jnp.bfloat16
    )
    space_inward, space_outward, time_inward, time_outward = lax.psum(
        (space_inward, space_outward, time_inward, time_outward), ("tm", "space")
    )
    factor = 1.0 / math.sqrt(frame_count * row_count * lax.axis_size("tm") * lax.axis_size("space"))
    project_grad = jnp.stack([space_inward, time_inward]) * factor
    combine_grad = jnp.stack([space_outward, time_outward]) * factor
    return (mixed_field, field_grad, project_grad, combine_grad)


def solution(mesh):
    in_specs = (P("tm", "space", None), P("tm", "space", None), P("tm", "space", None), P(), P())
    out_specs = (P("tm", "space", None), P("tm", "space", None), P(), P())
    return jax.shard_map(
        per_device, mesh=mesh, in_specs=in_specs, out_specs=out_specs, check_vma=False
    )
```

profile of v0, /device:TPU:2, one launch (start us, length us, event | category | flops | bytes accessed | tf_op | source)
XLA Modules:
  0.0 562.2 jit_solution(7572471238798868176)
XLA Ops:
  13.4 1.9 collective-permute-start.1
  15.3 2.4 collective-permute-start
  18.7 6.0 %all-to-all-start.2 = ((bf16[2,256,256]{2,0,1:T(2,128)(2,1)}), bf16[2,256,256]{2,0,1:T(2,128)(2,1)S(1)}, u32[]{:S(2)}, u32[]{:S(2)}) async-start(bf16[2,256,256]{2,0,1:T(2,128)(2,1)} %copy.163), calls=%async_computation.2 | async-start | bytes 524288 | tf_op jit(solution)/shard_map/all_to_all | solution.py:184
  26.2 8.0 %all-to-all-done.2 = bf16[2,256,256]{2,0,1:T(2,128)(2,1)S(1)} async-done(((bf16[2,256,256]{2,0,1:T(2,128)(2,1)}), bf16[2,256,256]{2,0,1:T(2,128)(2,1)S(1)}, u32[]{:S(2)}, u32[]{:S(2)}) %all-to-all-start.2) | async-done | bytes 262176 | tf_op jit(solution)/shard_map/all_to_all | solution.py:184
  34.3 3.1 pad_maximum_fusion.2
  37.3 2.1 reshape.238
  39.4 2.0 copy.145
  41.4 2.2 gather_fusion
  43.6 1.9 broadcast_select_fusion
  45.4 2.7 copy.146
  48.1 2.7 reshape.239
  54.0 6.7 %fusion.100 = (f32[4,8,128]{2,1,0:T(8,128)S(1)}, f32[4,8,128,512]{3,2,1,0:T(8,128)S(1)}) fusion(f32[4,8,128,512]{3,2,1,0:T(8,128)S(1)} %fusion.42), kind=kOutput, calls=%fused_computation.168 | output fusion | flops 8389119 | bytes 16793600 | tf_op jit(solution)/shard_map/while/body/eval_jaxpr/sub | solution.py:71
  61.5 2.0 copy-done
  63.4 1.5 fusion.30
  66.6 3.7 all-to-all-start
  72.0 8.0 %all-to-all-done = bf16[2,256,256]{2,0,1:T(2,128)(2,1)S(1)} async-done(((bf16[2,256,256]{2,0,1:T(2,128)(2,1)}), bf16[2,256,256]{2,0,1:T(2,128)(2,1)S(1)}, u32[]{:S(2)}, u32[]{:S(2)}) %all-to-all-start) | async-done | bytes 262176 | tf_op jit(solution)/shard_map/all_to_all | solution.py:183
  83.5 3.6 reshape.240
  87.1 2.7 slice_bitcast_fusion.3
  89.8 3.7 fusion.37
  93.5 3.3 divide_convert_fusion.1
  99.4 1.4 dot_general.98
  102.1 2.4 fusion.34
  106.5 11.7 %fusion.24 = bf16[16,32,1,8,32]{4,0,3,1,2:T(8,128)(2,1)S(1)} fusion(bf16[16,32,8,32]{3,2,1,0:T(8,128)(2,1)S(1)} %copy-done.8, bf16[8,16,16,32]{1,2,3,0:T(8,128)(2,1)S(1)} %fusion.15), kind=kOutput, calls=%fused_computation.45 | convolution fusion | flops 4325376 | bytes 655360 | tf_op jit(solution)/shard_map/hfgr,grhe->frhe/dot_general | solution.py:66
  119.8 2.8 convert_element_type.178
  122.6 2.8 convert_element_type.167
  126.6 2.0 convolution_bitcast_fusion.3
  128.7 2.5 convolution_bitcast_fusion.1
  133.0 3.4 all-to-all-start.3
  136.4 1.8 fusion.29
  138.3 6.9 %all-to-all-done.3 = bf16[16,32,256]{2,1,0:T(8,128)(2,1)S(1)} async-done(((bf16[16,32,256]{2,1,0:T(8,128)(2,1)}), bf16[16,32,256]{2,1,0:T(8,128)(2,1)S(1)}, u32[]{:S(2)}, u32[]{:S(2)}) %all-to-all-start.3) | async-done | bytes 262176 | tf_op jit(solution)/shard_map/all_to_all | solution.py:191
  145.1 4.0 all-to-all-start.1
  150.5 2.9 convolution_bitcast_fusion
  153.4 4.5 fusion.41
  158.0 11.7 %fusion.21 = f32[4,512,1,8,32]{1,4,3,0,2:T(8,128)} fusion(bf16[4,8,128,512]{3,2,1,0:T(8,128)(2,1)} %copy-done, f32[4,8,128,512]{3,2,1,0:T(8,128)} %fusion.41, bf16[4,128,8,32]{1,0,3,2:T(4,128)(2,1)S(1)} %copy-done.26), kind=kOutput, calls=%fused_computation.33 | convolution fusion | flops 148902400 | bytes 14942208 | tf_op jit(solution)/shard_map/while/body/eval_jaxpr/ghqk,gqhe->gkhe/dot_general | solution.py:66
  169.7 4.1 pad_maximum_fusion
  173.8 12.6 %copy.182 = f32[4,512,2,8,32]{4,3,2,1,0:T(8,128)} copy(f32[4,512,2,8,32]{1,4,3,0,2:T(8,128)} %pad_maximum_fusion) | data formatting | bytes 8388608 | tf_op jit(solution)/shard_map/while/body/eval_jaxpr/stack | solution.py:213
  186.4 16.9 %reshape.268 = f32[16,65536]{1,0:T(8,128)} reshape(f32[4,512,2,8,32]{4,3,2,1,0:T(8,128)} %copy.182) | data formatting | bytes 8388608 | tf_op jit(solution)/shard_map/while/body/eval_jaxpr/reshape | solution.py:213
  203.3 2.2 broadcast_in_dim.24
  205.5 38.1 %scatter_fusion = f32[12,65536]{1,0:T(8,128)} fusion(f32[12,65536]{1,0:T(8,128)} %broadcast_in_dim.24, s32[16]{0:T(128)S(1)} %fusion.91, f32[16,65536]{1,0:T(8,128)} %reshape.268), kind=kCustom, calls=%fused_computation.1 | custom fusion | flops 1048576 | bytes 12582976 | tf_op jit(solution)/shard_map/while/body/eval_jaxpr/scatter-add | solution.py:216
  243.6 2.8 reshape.246
  247.6 11.5 %fusion.31 = bf16[4,128,8,32]{1,3,2,0:T(8,128)(2,1)} fusion(bf16[4,8,128,512]{3,2,1,0:T(8,128)(2,1)} %copy-done, f32[4,8,128,512]{3,2,1,0:T(8,128)} %fusion.41, bf16[4,512,1,8,32]{1,0,4,3,2:T(4,128)(2,1)} %copy-done.6), kind=kOutput, calls=%fused_computation.62 | convolution fusion | flops 149033472 | bytes 13893632 | tf_op jit(solution)/shard_map/while/body/eval_jaxpr/ghqk,gkhe->gqhe/dot_general | solution.py:66
  259.1 2.2 collective-permute-start.2
  261.3 4.6 collective-permute-start.3
  265.9 2.0 convolution_bitcast_fusion.4
  267.8 1.7 copy.162
  271.9 2.0 fusion.70
  280.7 270.7 %all-reduce.3.cloned.1.call-done = (f32[1,256,768]{2,1,0:T(8,128)}, f32[1,256,768]{2,1,0:T(8,128)}, f32[1,256,256]{2,1,0:T(8,128)}, f32[1,256,256]{2,1,0:T(8,128)}) async-done(((f32[1,256,768]{2,1,0:T(8,128)}, f32[1,256,768]{2,1,0:T(8,128)}, f32[1,256,256]{2,1,0:T(8,128)}, f32[1,256,256]{2,1,0:T(8,128)}), (f32[1,256,768]{2,1,0:T(8,128)}, f32[1,256,768]{2,1,0:T(8,128)}, f32[1,256,256]{2,1,0:T(8,128)}, ...) | async-done | bytes 2097168 | tf_op jit(solution)/shard_map/psum | solution.py:238
  551.4 2.7 maximum_multiply_fusion
  (148 shorter events, 41.9 us)
Async XLA Ops:
  7.2 17.6 %copy-start.18 = (bf16[2,256,768]{2,1,0:T(8,128)(2,1)S(1)}, bf16[2,256,768]{2,1,0:T(8,128)(2,1)}, u32[]{:S(2)}) copy-start(bf16[2,256,768]{2,1,0:T(8,128)(2,1)} %param.10) | copy-start | bytes 2359300
  7.2 10.5 %copy-start.31 = (bf16[2,256,256]{2,1,0:T(8,128)(2,1)S(1)}, bf16[2,256,256]{2,1,0:T(8,128)(2,1)}, u32[]{:S(2)}) copy-start(bf16[2,256,256]{2,1,0:T(8,128)(2,1)} %param.8) | copy-start | bytes 786436
  8.4 17.1 %copy-start.34 = (s32[2,2,4]{2,1,0:T(2,128)S(1)}, s32[2,2,4]{2,1,0:T(2,128)}, u32[]{:S(2)}) copy-start(s32[2,2,4]{2,1,0:T(2,128)} %param.9) | copy-start | bytes 196
  10.8 0.7 copy-start.15
  13.4 20.9 %collective-permute-start.1 = (bf16[2,256,512]{1,0,2:T(2,128)(2,1)S(1)}, bf16[2,256,512]{1,0,2:T(2,128)(2,1)}, u32[]{:S(2)}, u32[]{:S(2)}) collective-permute-start(bf16[2,256,512]{1,0,2:T(2,128)(2,1)S(1)} %copy.194), channel_id=1, source_target_pairs={{1,0},{2,1},{3,2},{4,3},{5,4},{6,5},{7,6},{8,7},{9,8},{10,9},{11,1... | collective-permute-start | bytes 1572872 | tf_op jit(solution)/shard_map/ppermute | solution.py:23
  15.3 19.0 %collective-permute-start = (bf16[2,256,512]{1,0,2:T(2,128)(2,1)S(1)}, bf16[2,256,512]{1,0,2:T(2,128)(2,1)}, u32[]{:S(2)}, u32[]{:S(2)}) collective-permute-start(bf16[2,256,512]{1,0,2:T(2,128)(2,1)S(1)} %copy.194), channel_id=1, source_target_pairs={{0,1},{1,2},{2,3},{3,4},{4,5},{5,6},{6,7},{7,8},{8,9},{9,10},{10,1... | collective-permute-start | bytes 1572872 | tf_op jit(solution)/shard_map/ppermute | solution.py:21
  18.7 15.5 %all-to-all-start.2 = ((bf16[2,256,256]{2,0,1:T(2,128)(2,1)}), bf16[2,256,256]{2,0,1:T(2,128)(2,1)S(1)}, u32[]{:S(2)}, u32[]{:S(2)}) async-start(bf16[2,256,256]{2,0,1:T(2,128)(2,1)} %copy.163), calls=%async_computation.2 | async-start | bytes 524288 | tf_op jit(solution)/shard_map/all_to_all | solution.py:184
  26.2 25.5 %copy-start.25 = (bf16[4,128,8,32]{1,0,3,2:T(4,128)(2,1)}, bf16[4,128,8,32]{1,0,3,2:T(4,128)(2,1)S(1)}, u32[]{:S(2)}) copy-start(bf16[4,128,8,32]{1,0,3,2:T(4,128)(2,1)S(1)} %squeeze.57) | copy-start | bytes 786436
  34.2 36.1 %copy-start.11 = (bf16[2,8,32,256]{3,2,0,1:T(8,128)(2,1)}, bf16[2,8,32,256]{3,2,0,1:T(8,128)(2,1)S(1)}, u32[]{:S(2)}) copy-start(bf16[2,8,32,256]{3,2,0,1:T(8,128)(2,1)S(1)} %copy.164) | copy-start | bytes 786436
  51.7 1.0 copy-start.6
  51.7 9.8 %copy-start.1 = (bf16[4,512,1,8,32]{1,0,4,3,2:T(4,128)(2,1)}, bf16[4,512,1,8,32]{1,0,4,3,2:T(4,128)(2,1)S(1)}, u32[]{:S(2)}) copy-start(bf16[4,512,1,8,32]{1,0,4,3,2:T(4,128)(2,1)S(1)} %get-tuple-element.53) | copy-start | bytes 3145732
  61.4 2.0 copy-start
  63.4 1.9 copy-start.7
  63.4 1.9 copy-start.29
  65.2 16.3 %copy-start.22 = (bf16[4,128,8,32]{1,0,3,2:T(4,128)(2,1)}, bf16[4,128,8,32]{1,0,3,2:T(4,128)(2,1)S(1)}, u32[]{:S(2)}) copy-start(bf16[4,128,8,32]{1,0,3,2:T(4,128)(2,1)S(1)} %copy.151) | copy-start | bytes 786436
  65.4 16.9 %copy-start.19 = (bf16[2,256,768]{2,1,0:T(8,128)(2,1)S(1)}, bf16[2,256,768]{2,1,0:T(8,128)(2,1)}, u32[]{:S(2)}) copy-start(bf16[2,256,768]{2,1,0:T(8,128)(2,1)} %param.10) | copy-start | bytes 2359300
  66.6 13.4 %all-to-all-start = ((bf16[2,256,256]{2,0,1:T(2,128)(2,1)}), bf16[2,256,256]{2,0,1:T(2,128)(2,1)S(1)}, u32[]{:S(2)}, u32[]{:S(2)}) async-start(bf16[2,256,256]{2,0,1:T(2,128)(2,1)} %copy.153), calls=%async_computation | async-start | bytes 524288 | tf_op jit(solution)/shard_map/all_to_all | solution.py:183
  81.5 0.7 copy-start.23
  93.5 3.3 copy-start.10
  97.7 3.1 copy-start.3
  100.8 1.2 copy-start.17
  104.4 1.2 copy-start.9
  104.4 2.1 copy-start.8
  125.4 6.0 %copy-start.20 = (bf16[2,256,768]{2,1,0:T(8,128)(2,1)S(1)}, bf16[2,256,768]{2,1,0:T(8,128)(2,1)}, u32[]{:S(2)}) copy-start(bf16[2,256,768]{2,1,0:T(8,128)(2,1)} %param.10) | copy-start | bytes 2359300
  125.4 6.0 %copy-start.21 = (bf16[16,32,768]{2,1,0:T(8,128)(2,1)S(1)}, bf16[16,32,768]{2,1,0:T(8,128)(2,1)}, u32[]{:S(2)}) copy-start(bf16[16,32,768]{2,1,0:T(8,128)(2,1)} %convert_element_type.167) | copy-start | bytes 2359300
  126.6 5.3 copy-start.12
  131.2 5.2 copy-start.28
  131.9 18.1 %copy-start.30 = (bf16[2,256,256]{2,1,0:T(8,128)(2,1)S(1)}, bf16[2,256,256]{2,1,0:T(8,128)(2,1)}, u32[]{:S(2)}) copy-start(bf16[2,256,256]{2,1,0:T(8,128)(2,1)} %param.11) | copy-start | bytes 786436
  133.0 12.1 %all-to-all-start.3 = ((bf16[16,32,256]{2,1,0:T(8,128)(2,1)}), bf16[16,32,256]{2,1,0:T(8,128)(2,1)S(1)}, u32[]{:S(2)}, u32[]{:S(2)}) async-start(bf16[16,32,256]{2,1,0:T(8,128)(2,1)} %fusion.58), calls=%async_computation.3 | async-start | bytes 524288 | tf_op jit(solution)/shard_map/all_to_all | solution.py:191
  145.1 122.7 %all-to-all-start.1 = ((bf16[16,32,256]{2,1,0:T(8,128)(2,1)}), bf16[16,32,256]{2,1,0:T(8,128)(2,1)}, u32[]{:S(2)}, u32[]{:S(2)}) async-start(bf16[16,32,256]{2,1,0:T(8,128)(2,1)} %fusion.29), calls=%async_computation.1 | async-start | bytes 524288 | tf_op jit(solution)/shard_map/all_to_all | solution.py:190
  149.2 402.2 %all-reduce.3.cloned.1.call-start = ((), (), s32[]{:S(2)}) async-start(), calls=%async_computation.4 | async-start | bytes 4194304 | tf_op jit(solution)/shard_map/psum | solution.py:238
  149.3 0.7 copy-start.13
  150.4 3.0 copy-start.2
  153.4 4.5 copy-start.26
  259.1 14.8 %collective-permute-start.2 = (bf16[2,256,512]{2,1,0:T(8,128)(2,1)}, bf16[2,256,512]{2,1,0:T(8,128)(2,1)}, u32[]{:S(2)}, u32[]{:S(2)}) collective-permute-start(bf16[2,256,512]{2,1,0:T(8,128)(2,1)} %get-tuple-element.55), channel_id=1, source_target_pairs={{0,1},{1,2},{2,3},{3,4},{4,5},{5,6},{6,7},{7,8},{8,9},{9,10},{10,1... | collective-permute-start | bytes 1572872 | tf_op jit(solution)/shard_map/ppermute | solution.py:21
  261.3 12.6 %collective-permute-start.3 = (bf16[2,256,512]{2,1,0:T(8,128)(2,1)}, bf16[2,256,512]{2,1,0:T(8,128)(2,1)}, u32[]{:S(2)}, u32[]{:S(2)}) collective-permute-start(bf16[2,256,512]{2,1,0:T(8,128)(2,1)} %get-tuple-element.56), channel_id=1, source_target_pairs={{1,0},{2,1},{3,2},{4,3},{5,4},{6,5},{7,6},{8,7},{9,8},{10,9},{11,1... | collective-permute-start | bytes 1572872 | tf_op jit(solution)/shard_map/ppermute | solution.py:23
  269.5 6.8 %copy-start.16 = (bf16[2,256,256]{2,1,0:T(8,128)(2,1)S(1)}, bf16[2,256,256]{2,1,0:T(8,128)(2,1)}, u32[]{:S(2)}) copy-start(bf16[2,256,256]{2,1,0:T(8,128)(2,1)} %copy-done.15) | copy-start | bytes 786436
  275.3 1.0 copy-start.4
  276.3 1.7 copy-start.24
  276.3 1.7 copy-start.27
  277.0 1.6 copy-start.5
  277.0 2.6 copy-start.14
  551.4 2.7 copy-start.32
  551.4 2.7 copy-start.33
Sparse Core Ops, SparseCore 0:
  278.1 273.2 all-reduce.2
where the time goes:
time: 571 us; the launch traced here: 562 us
  waiting for transfers between devices  294 us (51%)
  local copies, waits for them, and re-layouts  81.3 us (14%)
  other arithmetic  73.3 us (13%)
  matrix products  70.6 us (12%)
  starting transfers between devices  28.3 us (5%)
  between operations  15.3 us (3%)
    psum x1, waiting for transfers between devices, per_device(): lax.psum((space_inward, space_outward, time_inward, time_outward), ('tm',...  271 us
    dot_general x12, matrix products, einsum_wide(): jnp.einsum(formula, left_op, right_op, preferred_element_type=jnp.float32)  53.7 us
    scatter-add x1, other arithmetic, backward_group(): return (running.at[group_rows].add(key_tiles), grad_query)  38.1 us
    reshape x1, local copies, waits for them, and re-layouts, backward_group(): jnp.stack([grad_keys, grad_values], axis=2)  16.9 us
    another operation x1, local copies, waits for them, and re-layouts, backward_group(): jnp.stack([grad_keys, grad_values], axis=2)  12.6 us
  transfers between devices with their start and end apart: 9, of which 4 were waited for; matrix products, arithmetic and copies ran while one was open for 22% of the time, Pallas kernels for 0%

commit v1 on v0

--- a/solution.py
+++ b/solution.py
@@ -1,3 +1,4 @@
+import functools
 import math
 import jax
 import jax.numpy as jnp
@@ -8,6 +9,13 @@
 BLOCK = 128
 HREACH = 2
 epsilon = 1e-05
+
+
+def work_levels_all_over_axis(buf, mesh_dim, mesh_name):
+    return lax.psum(lax.psum(buf, mesh_dim), mesh_name)
+
+
+assign_the_knots = functools.partial(work_levels_all_over_axis, mesh_dim="tm", mesh_name="space")
 
 
 def with_halo(cells, sides, width):
@@ -235,8 +243,8 @@
     field_grad = (mixed_grad.astype(jnp.float32) + norm_backward(act_grad, normed, inverse)).astype(
         jnp.bfloat16
     )
-    space_inward, space_outward, time_inward, time_outward = lax.psum(
-        (space_inward, space_outward, time_inward, time_outward), ("tm", "space")
+    space_inward, space_outward, time_inward, time_outward = assign_the_knots(
+        (space_inward, space_outward, time_inward, time_outward)
     )
     factor = 1.0 / math.sqrt(frame_count * row_count * lax.axis_size("tm") * lax.axis_size("space"))
     project_grad = jnp.stack([space_inward, time_inward]) * factor

time: 571 us -> 628 us (1.100)
  the two profiles are of different devices: /device:TPU:2 before, /device:TPU:1 now
where the time goes in v1:
time: 628 us; the launch traced here: 619 us
  waiting for transfers between devices  361 us (57%)
  local copies, waits for them, and re-layouts  79 us (13%)
  other arithmetic  72.7 us (12%)
  matrix products  61.5 us (10%)
  starting transfers between devices  29.2 us (5%)
  between operations  15.2 us (2%)
    psum x2, waiting for transfers between devices, work_levels_all_over_axis(): return lax.psum(lax.psum(buf, mesh_dim), mesh_name)  330 us
    dot_general x12, matrix products, einsum_wide(): jnp.einsum(formula, left_op, right_op, preferred_element_type=jnp.float32)  44.6 us
    scatter-add x1, other arithmetic, backward_group(): return (running.at[group_rows].add(key_tiles), grad_query)  37.6 us
    reshape x1, local copies, waits for them, and re-layouts, backward_group(): jnp.stack([grad_keys, grad_values], axis=2)  16.9 us
    another operation x1, local copies, waits for them, and re-layouts, backward_group(): jnp.stack([grad_keys, grad_values], axis=2)  12.8 us
  transfers between devices with their start and end apart: 10, of which 6 were waited for; matrix products, arithmetic and copies ran while one was open for 5% of the time, Pallas kernels for 0%

profile of v1, /device:TPU:1, one launch (start us, length us, event | category | flops | bytes accessed | tf_op | source)
XLA Modules:
  0.0 618.8 jit_solution(9270458105636629993)
XLA Ops:
  13.3 5.1 collective-permute-start.1
  18.4 1.9 collective-permute-start
  21.3 6.0 all-to-all-start.2
  28.0 10.6 %all-to-all-done.2 = bf16[2,256,256]{2,0,1:T(2,128)(2,1)S(1)} async-done(((bf16[2,256,256]{2,0,1:T(2,128)(2,1)}), bf16[2,256,256]{2,0,1:T(2,128)(2,1)S(1)}, u32[]{:S(2)}, u32[]{:S(2)}) %all-to-all-start.2) | async-done | bytes 262176 | tf_op jit(solution)/shard_map/all_to_all | solution.py:192
  38.6 2.9 pad_maximum_fusion.2
  41.5 2.1 reshape.238
  43.6 2.0 copy.145
  45.6 2.2 gather_fusion
  47.8 1.9 broadcast_select_fusion
  49.6 2.7 copy.146
  52.3 2.7 reshape.239
  58.1 6.7 %fusion.101 = (f32[4,8,128]{2,1,0:T(8,128)S(1)}, f32[4,8,128,512]{3,2,1,0:T(8,128)S(1)}) fusion(f32[4,8,128,512]{3,2,1,0:T(8,128)S(1)} %fusion.42), kind=kOutput, calls=%fused_computation.166 | output fusion | flops 8389119 | bytes 16793600 | tf_op jit(solution)/shard_map/while/body/eval_jaxpr/sub | solution.py:79
  65.6 1.9 copy-done
  67.6 1.5 fusion.30
  70.8 3.6 all-to-all-start
  76.1 7.4 %all-to-all-done = bf16[2,256,256]{2,0,1:T(2,128)(2,1)S(1)} async-done(((bf16[2,256,256]{2,0,1:T(2,128)(2,1)}), bf16[2,256,256]{2,0,1:T(2,128)(2,1)S(1)}, u32[]{:S(2)}, u32[]{:S(2)}) %all-to-all-start) | async-done | bytes 262176 | tf_op jit(solution)/shard_map/all_to_all | solution.py:191
  87.0 3.6 reshape.240
  90.6 2.7 slice_bitcast_fusion.3
  93.3 3.7 fusion.37
  97.0 3.4 divide_convert_fusion.1
  100.5 2.4 fusion.34
  107.7 3.2 convert_element_type.178
  111.0 2.8 convert_element_type.167
  114.9 2.5 fusion.23
  119.2 2.5 fusion.105
  123.5 3.4 all-to-all-start.3
  127.0 1.9 fusion.106
  128.9 6.4 %all-to-all-done.3 = bf16[16,32,256]{2,1,0:T(8,128)(2,1)S(1)} async-done(((bf16[16,32,256]{2,1,0:T(8,128)(2,1)}), bf16[16,32,256]{2,1,0:T(8,128)(2,1)S(1)}, u32[]{:S(2)}, u32[]{:S(2)}) %all-to-all-start.3) | async-done | bytes 262176 | tf_op jit(solution)/shard_map/all_to_all | solution.py:199
  137.5 2.9 convolution_bitcast_fusion
  140.4 4.5 fusion.41
  145.0 11.7 %fusion.21 = f32[4,512,1,8,32]{1,4,3,0,2:T(8,128)} fusion(bf16[4,8,128,512]{3,2,1,0:T(8,128)(2,1)} %copy-done, f32[4,8,128,512]{3,2,1,0:T(8,128)} %fusion.41, bf16[4,128,8,32]{1,0,3,2:T(4,128)(2,1)S(1)} %copy-done.31), kind=kOutput, calls=%fused_computation.33 | convolution fusion | flops 148902400 | bytes 14942208 | tf_op jit(solution)/shard_map/while/body/eval_jaxpr/ghqk,gqhe->gkhe/dot_general | solution.py:74
  156.7 4.2 pad_maximum_fusion
  160.8 12.8 %copy.182 = f32[4,512,2,8,32]{4,3,2,1,0:T(8,128)} copy(f32[4,512,2,8,32]{1,4,3,0,2:T(8,128)} %pad_maximum_fusion) | data formatting | bytes 8388608 | tf_op jit(solution)/shard_map/while/body/eval_jaxpr/stack | solution.py:221
  173.6 16.9 %reshape.268 = f32[16,65536]{1,0:T(8,128)} reshape(f32[4,512,2,8,32]{4,3,2,1,0:T(8,128)} %copy.182) | data formatting | bytes 8388608 | tf_op jit(solution)/shard_map/while/body/eval_jaxpr/reshape | solution.py:221
  190.4 2.2 broadcast_in_dim.24
  192.7 37.6 %scatter_fusion = f32[12,65536]{1,0:T(8,128)} fusion(f32[12,65536]{1,0:T(8,128)} %broadcast_in_dim.24, s32[16]{0:T(128)S(1)} %fusion.92, f32[16,65536]{1,0:T(8,128)} %reshape.268), kind=kCustom, calls=%fused_computation.1 | custom fusion | flops 1048576 | bytes 12582976 | tf_op jit(solution)/shard_map/while/body/eval_jaxpr/scatter-add | solution.py:224
  230.3 2.8 reshape.246
  234.4 1.9 collective-permute-start.2
  236.3 3.4 collective-permute-start.3
  239.8 11.5 %fusion.31 = bf16[4,128,8,32]{1,3,2,0:T(8,128)(2,1)} fusion(bf16[4,8,128,512]{3,2,1,0:T(8,128)(2,1)} %copy-done, f32[4,8,128,512]{3,2,1,0:T(8,128)} %fusion.41, bf16[4,512,1,8,32]{1,0,4,3,2:T(4,128)(2,1)} %copy-done.10), kind=kOutput, calls=%fused_computation.59 | convolution fusion | flops 149033472 | bytes 13893632 | tf_op jit(solution)/shard_map/while/body/eval_jaxpr/ghqk,gkhe->gqhe/dot_general | solution.py:74
  252.5 2.1 fusion.66
  259.9 112.4 %all-reduce.7.cloned.1.call-done = (f32[256,768]{1,0:T(8,128)}, f32[256,768]{1,0:T(8,128)}, f32[256,256]{1,0:T(8,128)}, f32[256,256]{1,0:T(8,128)}) async-done(((f32[256,768]{1,0:T(8,128)}, f32[256,768]{1,0:T(8,128)}, f32[256,256]{1,0:T(8,128)}, f32[256,256]{1,0:T(8,128)}), (f32[256,768]{1,0:T(8,128)}, f32[256,768]{1,0:T(8,128)}, f32[256,256]{1,0:T(8,128)}, ...) | async-done | bytes 2097168 | tf_op jit(solution)/shard_map/psum | solution.py:15
  373.2 1.8 fusion.29
  375.0 3.8 all-to-all-start.1
  379.8 6.6 %all-to-all-done.1 = bf16[16,32,256]{2,1,0:T(8,128)(2,1)S(1)} async-done(((bf16[16,32,256]{2,1,0:T(8,128)(2,1)}), bf16[16,32,256]{2,1,0:T(8,128)(2,1)S(1)}, u32[]{:S(2)}, u32[]{:S(2)}) %all-to-all-start.1) | async-done | bytes 262176 | tf_op jit(solution)/shard_map/all_to_all | solution.py:198
  387.4 1.7 fusion.102
  390.5 217.7 %all-reduce.5.cloned.1.call-done = (f32[1,256,768]{2,1,0:T(8,128)}, f32[1,256,768]{2,1,0:T(8,128)}, f32[1,256,256]{2,1,0:T(8,128)}, f32[1,256,256]{2,1,0:T(8,128)}) async-done(((f32[1,256,768]{2,1,0:T(8,128)}, f32[1,256,768]{2,1,0:T(8,128)}, f32[1,256,256]{2,1,0:T(8,128)}, f32[1,256,256]{2,1,0:T(8,128)}), (f32[1,256,768]{2,1,0:T(8,128)}, f32[1,256,768]{2,1,0:T(8,128)}, f32[1,256,256]{2,1,0:T(8,128)}, ...) | async-done | bytes 2097168 | tf_op jit(solution)/shard_map/psum | solution.py:15
  608.2 2.7 maximum_multiply_fusion
  (157 shorter events, 42.7 us)
Async XLA Ops:
  7.2 13.2 %copy-start.34 = (bf16[2,256,256]{2,1,0:T(8,128)(2,1)S(1)}, bf16[2,256,256]{2,1,0:T(8,128)(2,1)}, u32[]{:S(2)}) copy-start(bf16[2,256,256]{2,1,0:T(8,128)(2,1)} %param.8) | copy-start | bytes 786436
  7.2 20.1 %copy-start.37 = (s32[2,2,4]{2,1,0:T(2,128)S(1)}, s32[2,2,4]{2,1,0:T(2,128)}, u32[]{:S(2)}) copy-start(s32[2,2,4]{2,1,0:T(2,128)} %param.9) | copy-start | bytes 196
  10.7 0.7 copy-start.19
  13.3 25.3 %collective-permute-start.1 = (bf16[2,256,512]{1,0,2:T(2,128)(2,1)S(1)}, bf16[2,256,512]{1,0,2:T(2,128)(2,1)S(1)}, u32[]{:S(2)}, u32[]{:S(2)}) collective-permute-start(bf16[2,256,512]{1,0,2:T(2,128)(2,1)S(1)} %copy.194), channel_id=1, source_target_pairs={{1,0},{2,1},{3,2},{4,3},{5,4},{6,5},{7,6},{8,7},{9,8},{10,9},{11,1... | collective-permute-start | bytes 1572872 | tf_op jit(solution)/shard_map/ppermute | solution.py:31
  18.4 20.2 %collective-permute-start = (bf16[2,256,512]{1,0,2:T(2,128)(2,1)S(1)}, bf16[2,256,512]{1,0,2:T(2,128)(2,1)}, u32[]{:S(2)}, u32[]{:S(2)}) collective-permute-start(bf16[2,256,512]{1,0,2:T(2,128)(2,1)S(1)} %copy.194), channel_id=1, source_target_pairs={{0,1},{1,2},{2,3},{3,4},{4,5},{5,6},{6,7},{7,8},{8,9},{9,10},{10,1... | collective-permute-start | bytes 1572872 | tf_op jit(solution)/shard_map/ppermute | solution.py:29
  21.3 17.3 %all-to-all-start.2 = ((bf16[2,256,256]{2,0,1:T(2,128)(2,1)}), bf16[2,256,256]{2,0,1:T(2,128)(2,1)S(1)}, u32[]{:S(2)}, u32[]{:S(2)}) async-start(bf16[2,256,256]{2,0,1:T(2,128)(2,1)} %copy.163), calls=%async_computation.2 | async-start | bytes 524288 | tf_op jit(solution)/shard_map/all_to_all | solution.py:192
  28.0 27.9 %copy-start.30 = (bf16[4,128,8,32]{1,0,3,2:T(4,128)(2,1)}, bf16[4,128,8,32]{1,0,3,2:T(4,128)(2,1)S(1)}, u32[]{:S(2)}) copy-start(bf16[4,128,8,32]{1,0,3,2:T(4,128)(2,1)S(1)} %squeeze.57) | copy-start | bytes 786436
  38.6 35.8 %copy-start.15 = (bf16[2,8,32,256]{3,2,0,1:T(8,128)(2,1)}, bf16[2,8,32,256]{3,2,0,1:T(8,128)(2,1)S(1)}, u32[]{:S(2)}) copy-start(bf16[2,8,32,256]{3,2,0,1:T(8,128)(2,1)S(1)} %copy.164) | copy-start | bytes 786436
  55.8 1.0 copy-start.10
  55.9 9.8 %copy-start.1 = (bf16[4,512,1,8,32]{1,0,4,3,2:T(4,128)(2,1)}, bf16[4,512,1,8,32]{1,0,4,3,2:T(4,128)(2,1)S(1)}, u32[]{:S(2)}) copy-start(bf16[4,512,1,8,32]{1,0,4,3,2:T(4,128)(2,1)S(1)} %get-tuple-element.57) | copy-start | bytes 3145732
  65.6 2.0 copy-start
  67.6 1.9 copy-start.11
  67.6 1.9 copy-start.33
  69.3 15.6 %copy-start.27 = (bf16[4,128,8,32]{1,0,3,2:T(4,128)(2,1)}, bf16[4,128,8,32]{1,0,3,2:T(4,128)(2,1)S(1)}, u32[]{:S(2)}) copy-start(bf16[4,128,8,32]{1,0,3,2:T(4,128)(2,1)S(1)} %copy.151) | copy-start | bytes 786436
  69.5 16.2 %copy-start.22 = (bf16[2,256,768]{2,1,0:T(8,128)(2,1)S(1)}, bf16[2,256,768]{2,1,0:T(8,128)(2,1)}, u32[]{:S(2)}) copy-start(bf16[2,256,768]{2,1,0:T(8,128)(2,1)} %param.10) | copy-start | bytes 2359300
  70.8 12.6 %all-to-all-start = ((bf16[2,256,256]{2,0,1:T(2,128)(2,1)}), bf16[2,256,256]{2,0,1:T(2,128)(2,1)S(1)}, u32[]{:S(2)}, u32[]{:S(2)}) async-start(bf16[2,256,256]{2,0,1:T(2,128)(2,1)} %copy.153), calls=%async_computation | async-start | bytes 524288 | tf_op jit(solution)/shard_map/all_to_all | solution.py:191
  85.0 0.7 copy-start.28
  97.0 3.4 copy-start.5
  97.0 3.4 copy-start.21
  100.4 3.2 copy-start.12
  102.8 1.6 copy-start.14
  103.7 1.6 copy-start.13
  114.8 7.6 %copy-start.8 = (f32[8,2,32,256]{3,2,1,0:T(8,128)}, f32[8,2,32,256]{3,2,1,0:T(8,128)S(1)}, u32[]{:S(2)}) copy-start(f32[8,2,32,256]{3,2,1,0:T(8,128)S(1)} %copy.155) | copy-start | bytes 1572868
  114.9 4.3 copy-start.29
  117.7 4.7 copy-start.3
  117.7 4.2 copy-start.23
  117.7 4.7 copy-start.16
  119.2 2.7 copy-start.24
  123.5 11.8 %all-to-all-start.3 = ((bf16[16,32,256]{2,1,0:T(8,128)(2,1)}), bf16[16,32,256]{2,1,0:T(8,128)(2,1)S(1)}, u32[]{:S(2)}, u32[]{:S(2)}) async-start(bf16[16,32,256]{2,1,0:T(8,128)(2,1)} %fusion.58), calls=%async_computation.3 | async-start | bytes 524288 | tf_op jit(solution)/shard_map/all_to_all | solution.py:199
  126.9 245.5 %all-reduce.7.cloned.1.call-start = ((), (), s32[]{:S(2)}) async-start(), calls=%async_computation.5 | async-start | bytes 4194304 | tf_op jit(solution)/shard_map/psum | solution.py:15
  135.3 0.7 copy-start.17
  137.4 3.0 copy-start.2
  140.4 4.5 copy-start.31
  234.4 21.4 %collective-permute-start.2 = (bf16[2,256,512]{2,1,0:T(8,128)(2,1)}, bf16[2,256,512]{2,1,0:T(8,128)(2,1)}, u32[]{:S(2)}, u32[]{:S(2)}) collective-permute-start(bf16[2,256,512]{2,1,0:T(8,128)(2,1)} %get-tuple-element.59), channel_id=1, source_target_pairs={{0,1},{1,2},{2,3},{3,4},{4,5},{5,6},{6,7},{7,8},{8,9},{9,10},{10,1... | collective-permute-start | bytes 1572872 | tf_op jit(solution)/shard_map/ppermute | solution.py:29
  236.3 19.5 %collective-permute-start.3 = (bf16[2,256,512]{2,1,0:T(8,128)(2,1)}, bf16[2,256,512]{2,1,0:T(8,128)(2,1)}, u32[]{:S(2)}, u32[]{:S(2)}) collective-permute-start(bf16[2,256,512]{2,1,0:T(8,128)(2,1)} %get-tuple-element.60), channel_id=1, source_target_pairs={{1,0},{2,1},{3,2},{4,3},{5,4},{6,5},{7,6},{8,7},{9,8},{10,9},{11,1... | collective-permute-start | bytes 1572872 | tf_op jit(solution)/shard_map/ppermute | solution.py:31
  251.3 6.9 %copy-start.20 = (bf16[2,256,256]{2,1,0:T(8,128)(2,1)S(1)}, bf16[2,256,256]{2,1,0:T(8,128)(2,1)}, u32[]{:S(2)}) copy-start(bf16[2,256,256]{2,1,0:T(8,128)(2,1)} %copy-done.19) | copy-start | bytes 786436
  252.5 3.3 copy-start.25
  257.2 1.0 copy-start.6
  258.9 113.5 %copy-start.4 = (bf16[16,32,8,32]{3,2,1,0:T(8,128)(2,1)S(1)}, bf16[16,32,8,32]{3,2,1,0:T(8,128)(2,1)}, u32[]{:S(2)}) copy-start(bf16[16,32,8,32]{3,2,1,0:T(8,128)(2,1)} %copy-done.3) | copy-start | bytes 786436
  259.9 113.3 %copy-start.9 = (f32[8,2,32,256]{3,2,1,0:T(8,128)S(1)}, f32[8,2,32,256]{3,2,1,0:T(8,128)}, u32[]{:S(2)}) copy-start(f32[8,2,32,256]{3,2,1,0:T(8,128)} %copy-done.8) | copy-start | bytes 1572868
  259.9 348.3 %all-reduce.5.cloned.1.call-start = ((), (), s32[]{:S(2)}) async-start(), calls=%async_computation.4 | async-start | bytes 4194304 | tf_op jit(solution)/shard_map/psum | solution.py:15
  372.4 14.7 %copy-start.26 = (bf16[4,128,8,32]{1,0,3,2:T(4,128)(2,1)S(1)}, bf16[4,128,8,32]{1,0,3,2:T(4,128)(2,1)}, u32[]{:S(2)}) copy-start(bf16[4,128,8,32]{1,0,3,2:T(4,128)(2,1)} %copy-done.25) | copy-start | bytes 786436
  372.4 15.0 %copy-start.7 = (f32[2,256,512]{2,1,0:T(8,128)S(1)}, f32[2,256,512]{2,1,0:T(8,128)}, u32[]{:S(2)}) copy-start(f32[2,256,512]{2,1,0:T(8,128)} %copy-done.6) | copy-start | bytes 3145732
  375.0 14.4 %copy-start.18 = (bf16[8,2,32,256]{3,2,0,1:T(8,128)(2,1)S(1)}, bf16[8,2,32,256]{3,2,0,1:T(8,128)(2,1)}, u32[]{:S(2)}) copy-start(bf16[8,2,32,256]{3,2,0,1:T(8,128)(2,1)} %copy-done.17) | copy-start | bytes 786436
  375.0 11.4 %all-to-all-start.1 = ((bf16[16,32,256]{2,1,0:T(8,128)(2,1)}), bf16[16,32,256]{2,1,0:T(8,128)(2,1)S(1)}, u32[]{:S(2)}, u32[]{:S(2)}) async-start(bf16[16,32,256]{2,1,0:T(8,128)(2,1)} %fusion.29), calls=%async_computation.1 | async-start | bytes 524288 | tf_op jit(solution)/shard_map/all_to_all | solution.py:198
  379.8 7.6 %copy-start.32 = (bf16[256,768]{1,0:T(8,128)(2,1)}, bf16[256,768]{1,0:T(8,128)(2,1)S(1)}, u32[]{:S(2)}) copy-start(bf16[256,768]{1,0:T(8,128)(2,1)S(1)} %slice_bitcast_fusion) | copy-start | bytes 1179652
  608.2 2.7 copy-start.35
  608.2 2.7 copy-start.36
Sparse Core Ops, SparseCore 0:
  260.0 112.3 all-reduce.6
  375.2 232.9 all-reduce.4
